TPU v7x, 1024 devices: a whole 8x8x8 slice. The times are simulated.
1024 devices in a mesh: head: 8 (over y), inner: 8 (over z_hi, core), outer: 16 (over z_lo, x).
Axes of the slice: x: 8, y: 8, z: 8 (z_hi: 4, z_lo: 2; z = z_hi * 2 + z_lo), core: 2. Of those that a mesh axis runs over, the one named last changes fastest.
Arguments:
- queries: bfloat16 [49152, 8192], P(('inner', 'outer', 'head')), may hold values from -30 to 30
- keys: bfloat16 [49152, 1024], P(('inner', 'outer', 'head')), may hold values from -30 to 30
- values: bfloat16 [49152, 1024], P(('inner', 'outer', 'head')), may hold values from -6 to 6
- positions: int32 [49152], replicated, may hold values from 0 to 49151, as said below
- plan: int32 [128, 3], replicated, may hold values 0 or 1
Outputs:
- attention: bfloat16 [49152, 8192], P(('inner', 'outer', 'head'))
- log_sum: float32 [64, 49152], P('head', ('inner', 'outer'))
Inputs may be any that keep to these rules, and one draw needn't show every extreme that they name: Every position 0 to 49151 appears once; each aligned run of 192 rows holds consecutive positions in increasing order.
All inputs are finite; a program needn't handle non-finite values.
Results may differ from a plain program's by a relative error of at most 0.0039.
Values may be sent and summed in bfloat16 or wider, within the bound.
A program may use at most 32 MiB of HBM per device.

v0:
```python
import jax
import jax.numpy as jnp
from jax import lax
from jax.sharding import PartitionSpec as P

QUERY_HEADS = 64
KEY_VALUE_HEADS = 8
HEAD_WIDTH = 128


def passed_along(value, axis, by):
    devices = lax.axis_size(axis)
    return lax.ppermute(value, axis, [(i, (i + by) % devices) for i in range(devices)])


def key_blocks(here, inner_count, outer_count):
    inner_here = here // outer_count
    outer_here = here % outer_count
    first = (inner_here - 1) % inner_count * outer_count + outer_here
    second = (inner_here - 2) % inner_count * outer_count + outer_here
    third = inner_here * outer_count + (outer_here - 1) % outer_count
    return (here, first, second, third)


def visible_mask(positions, plan, sources, here, block_rows):
    table = positions.reshape(-1, block_rows)
    query_place = table[here]
    key_place = jnp.concatenate([table[source] for source in sources])
    flags = jnp.concatenate([jnp.ones((1,), jnp.int32), plan[here]])
    step_used = jnp.repeat(flags, block_rows)
    return (key_place[None, :] <= query_place[:, None]) & (step_used[None, :] == 1)


def attend_window(
    query_head_stack, key_head_stack, value_head_stack, causal_mask, group, head_size
):

    def one_head(index):
        query_now = query_head_stack[index]
        key_now = key_head_stack[index // group]
        value_now = value_head_stack[index // group]
        scores = lax.dot_general(
            query_now, key_now, (((1,), (1,)), ((), ())), preferred_element_type=jnp.float32
        )
        scores = scores * head_size ** (-0.5)
        scores = jnp.where(causal_mask, scores, -jnp.inf)
        top = jnp.max(scores, axis=1, keepdims=True)
        weights = jnp.exp(scores - top)
        total = jnp.sum(weights, axis=1, keepdims=True)
        mixed_output = jnp.dot(
            weights.astype(jnp.bfloat16), value_now, preferred_element_type=jnp.float32
        )
        return ((mixed_output / total).astype(jnp.bfloat16), (top + jnp.log(total))[:, 0])

    return lax.map(one_head, jnp.arange(query_head_stack.shape[0], dtype=jnp.int32))


def per_device(queries, keys, values, positions, plan):
    inner_count = lax.axis_size("inner")
    outer_count = lax.axis_size("outer")
    here = lax.axis_index("inner") * outer_count + lax.axis_index("outer")
    paired = jnp.stack((keys, values))

    def pass_inner(block_data):
        return passed_along(block_data, "inner", 1)

    grouped, pairs = (
        lax.all_to_all(queries[None], "head", split_axis=2, concat_axis=1, tiled=True),
        lax.all_to_all(paired, "head", split_axis=2, concat_axis=1, tiled=True),
    )
    first = pass_inner(pairs)
    second = pass_inner(first)
    third = passed_along(pairs, "outer", 1)
    gathered = jnp.stack((pairs, first, second, third))
    block_rows = grouped.shape[1]
    query_head_stack = grouped[0].reshape(block_rows, -1, HEAD_WIDTH).transpose(1, 0, 2)
    key_head_stack = gathered[:, 0].reshape(4 * block_rows, -1, HEAD_WIDTH).transpose(1, 0, 2)
    value_head_stack = gathered[:, 1].reshape(4 * block_rows, -1, HEAD_WIDTH).transpose(1, 0, 2)
    sources = key_blocks(here, inner_count, outer_count)
    causal_mask = visible_mask(positions, plan, sources, here, block_rows)
    mixed_output, hidden_states = attend_window(
        query_head_stack,
        key_head_stack,
        value_head_stack,
        causal_mask,
        QUERY_HEADS // KEY_VALUE_HEADS,
        HEAD_WIDTH,
    )
    rows_out = mixed_output.transpose(1, 0, 2).reshape(block_rows, -1)
    returned = lax.all_to_all(rows_out, "head", split_axis=0, concat_axis=1, tiled=True)
    return (returned, hidden_states)


def solution(mesh):
    in_specs = (
        P(("inner", "outer", "head"), None),
        P(("inner", "outer", "head"), None),
        P(("inner", "outer", "head"), None),
        P(),
        P(),
    )
    out_specs = (P(("inner", "outer", "head"), None), P("head", ("inner", "outer")))
    return jax.shard_map(
        per_device, mesh=mesh, in_specs=in_specs, out_specs=out_specs, check_vma=False
    )
```

profile of v0, /device:TPU:128, one launch (start us, length us, event | category | flops | bytes accessed | tf_op | source)
XLA Modules:
  0.0 204.6 jit_solution(4190646587786312622)
XLA Ops:
  0.7 1.0 pad_maximum_fusion.1
  2.1 1.4 reshape.56
  3.5 7.6 %all-to-all-start.1 = ((bf16[8,2,6144]{2,1,0:T(2,128)(2,1)}), bf16[8,2,6144]{2,1,0:T(2,128)(2,1)S(1)}, u32[]{:S(2)}, u32[]{:S(2)}) async-start(bf16[8,2,6144]{2,1,0:T(2,128)(2,1)} %reshape.56), calls=%async_computation.1 | async-start | bytes 393216 | tf_op jit(solution)/shard_map/all_to_all | solution.py:69
  11.1 6.8 %copy.42 = bf16[1,48,8192]{1,0,2:T(2,128)(2,1)} copy(bf16[1,48,8192]{2,1,0:T(8,128)(2,1)S(1)} %bitcast.76) | data formatting | bytes 1572864 | tf_op jit(solution)/shard_map/broadcast_in_dim | solution.py:68
  17.9 0.5 broadcast.28
  18.4 45.2 %reduce.10 = bf16[8192,48]{1,0:T(8,128)(2,1)S(1)} reduce(bf16[8192,1,48]{2,1,0:T(2,128)(2,1)} %bitcast.66, bf16[]{:T(256)} %broadcast.28), dimensions={1}, to_apply=%bitcast.47.reduce_sub_computation | reduce | bytes 1572866
  63.6 4.0 %reshape.54 = bf16[8,2,24576]{2,1,0:T(2,128)(2,1)} reshape(bf16[8192,48]{1,0:T(8,128)(2,1)S(1)} %reduce.10) | data formatting | bytes 1572864
  67.7 7.2 %all-to-all-start = ((bf16[8,2,24576]{2,1,0:T(2,128)(2,1)}), bf16[8,2,24576]{2,1,0:T(2,128)(2,1)S(1)}, u32[]{:S(2)}, u32[]{:S(2)}) async-start(bf16[8,2,24576]{2,1,0:T(2,128)(2,1)} %reshape.54), calls=%async_computation | async-start | bytes 1572864 | tf_op jit(solution)/shard_map/all_to_all | solution.py:68
  74.8 0.5 reshape.57
  75.8 1.9 collective-permute-start
  78.0 3.4 %collective-permute-start.2 = (bf16[2,384,128]{2,1,0:T(8,128)(2,1)S(1)}, bf16[2,384,128]{2,1,0:T(8,128)(2,1)S(1)}, u32[]{:S(2)}, u32[]{:S(2)}) collective-permute-start(bf16[2,384,128]{2,1,0:T(8,128)(2,1)S(1)} %bitcast.80), channel_id=1, source_target_pairs={{0,1},{1,2},{2,3},{3,4},{4,5},{5,6},{6,7},{7,8},{8,9},{9,10},{10,1... | collective-permute-start | bytes 589832 | tf_op jit(solution)/shard_map/ppermute | solution.py:13
  81.4 13.6 %collective-permute-done = bf16[2,384,128]{2,1,0:T(8,128)(2,1)S(1)} collective-permute-done((bf16[2,384,128]{2,1,0:T(8,128)(2,1)S(1)}, bf16[2,384,128]{2,1,0:T(8,128)(2,1)S(1)}, u32[]{:S(2)}, u32[]{:S(2)}) %collective-permute-start) | collective-permute-done | bytes 196640 | tf_op jit(solution)/shard_map/ppermute | solution.py:13
  95.1 2.1 %collective-permute-start.1 = (bf16[2,384,128]{2,1,0:T(8,128)(2,1)S(1)}, bf16[2,384,128]{2,1,0:T(8,128)(2,1)S(1)}, u32[]{:S(2)}, u32[]{:S(2)}) collective-permute-start(bf16[2,384,128]{2,1,0:T(8,128)(2,1)S(1)} %collective-permute-done), channel_id=1, source_target_pairs={{0,16},{16,32},{32,48},{48,64},{64,80},{80,96},{96,112},{112,0},{1... | collective-permute-start | bytes 589832 | tf_op jit(solution)/shard_map/ppermute | solution.py:13
  97.3 0.6 eq.22
  97.9 0.6 dynamic-slice_reduce_fusion.3
  98.5 1.3 pad_add_fusion
  99.8 5.5 %collective-permute-done.1 = bf16[2,384,128]{2,1,0:T(8,128)(2,1)S(1)} collective-permute-done((bf16[2,384,128]{2,1,0:T(8,128)(2,1)S(1)}, bf16[2,384,128]{2,1,0:T(8,128)(2,1)S(1)}, u32[]{:S(2)}, u32[]{:S(2)}) %collective-permute-start.1) | collective-permute-done | bytes 196640 | tf_op jit(solution)/shard_map/ppermute | solution.py:13
  105.4 0.8 fusion.26
  106.2 5.4 %reshape.55 = bf16[8192,1,48]{2,1,0:T(2,128)(2,1)} reshape(bf16[8,2,24576]{2,1,0:T(2,128)(2,1)S(1)} %all-to-all-done) | data formatting | bytes 1572864
  111.6 8.1 %copy.43 = bf16[1,48,8192]{2,1,0:T(8,128)(2,1)S(1)} copy(bf16[1,48,8192]{1,0,2:T(2,128)(2,1)} %bitcast.67) | data formatting | bytes 1572864 | tf_op jit(solution)/shard_map/all_to_all | solution.py:68
  120.8 1.0 copy.49
  121.8 0.6 iota.3
  122.4 57.0 %while.13 = (s32[]{:T(128)}, bf16[8,384,128]{2,1,0:T(8,128)(2,1)S(1)}, f32[8,384]{1,0:T(8,128)}, s32[8]{0:T(128)}, bf16[8,384,128]{2,1,0:T(8,128)(2,1)}, /*index...) while((s32[]{:T(128)}, ...), condition=%wide.region_3.4_spmd.clone, body=%wide.region_0.3_spmd.clone.sunk | while | flops 307396224 | bytes 8092855 | solution.py:55
  122.4 1.3 dynamic_slice.46
  125.4 1.8 fusion.34
  127.2 0.5 fusion.35
  127.6 1.3 dynamic_update_slice.14
  129.0 0.6 fusion.36
  129.6 1.3 dynamic_slice.46
  132.5 1.8 fusion.34
  134.3 0.5 fusion.35
  134.8 1.3 dynamic_update_slice.14
  136.1 0.6 fusion.36
  136.7 1.3 dynamic_slice.46
  139.6 1.8 fusion.34
  141.4 0.5 fusion.35
  141.9 1.3 dynamic_update_slice.14
  143.2 0.6 fusion.36
  143.8 1.3 dynamic_slice.46
  146.7 1.8 fusion.34
  148.5 0.5 fusion.35
  149.0 1.3 dynamic_update_slice.14
  150.3 0.6 fusion.36
  150.9 1.3 dynamic_slice.46
  153.9 1.8 fusion.34
  156.1 1.3 dynamic_update_slice.14
  157.5 0.6 fusion.36
  158.1 1.3 dynamic_slice.46
  161.0 1.8 fusion.34
  162.8 0.5 fusion.35
  163.3 1.3 dynamic_update_slice.14
  164.6 0.6 fusion.36
  165.2 1.3 dynamic_slice.46
  168.1 1.8 fusion.34
  170.4 1.3 dynamic_update_slice.14
  171.7 0.6 fusion.36
  172.3 1.3 dynamic_slice.46
  175.2 1.8 fusion.34
  177.0 0.5 fusion.35
  177.5 1.3 dynamic_update_slice.14
  178.8 0.6 fusion.36
  179.4 0.5 copy.50
  180.3 23.4 %all_to_all.52 = bf16[8,48,1024]{2,1,0:T(8,128)(2,1)S(1)} all-to-all(bf16[8,48,1024]{2,1,0:T(8,128)(2,1)S(1)} %all_to_all.45), channel_id=1, replica_groups=mesh['head'=8,'inner'=8,'outer'=16] {'head'}, dimensions={0} | all-to-all | bytes 1572864 | tf_op jit(solution)/shard_map/all_to_all | solution.py:90
  203.7 0.9 copy.55
  (41 shorter events, 3.8 us)
Async XLA Ops:
  0.6 77.2 %copy-start = (s32[128,3]{0,1:T(4,128)S(1)}, s32[128,3]{0,1:T(4,128)}, u32[]{:S(2)}) copy-start(s32[128,3]{0,1:T(4,128)} %param.11) | copy-start | bytes 4612
  0.6 10.5 %copy-start.1 = (bf16[48,8192]{1,0:T(8,128)(2,1)S(1)}, bf16[48,8192]{1,0:T(8,128)(2,1)}, u32[]{:S(2)}) copy-start(bf16[48,8192]{1,0:T(8,128)(2,1)} %param.7) | copy-start | bytes 2359300
  3.5 64.1 %all-to-all-start.1 = ((bf16[8,2,6144]{2,1,0:T(2,128)(2,1)}), bf16[8,2,6144]{2,1,0:T(2,128)(2,1)S(1)}, u32[]{:S(2)}, u32[]{:S(2)}) async-start(bf16[8,2,6144]{2,1,0:T(2,128)(2,1)} %reshape.56), calls=%async_computation.1 | async-start | bytes 393216 | tf_op jit(solution)/shard_map/all_to_all | solution.py:69
  63.6 14.2 %copy-start.2 = (s32[49152]{0:T(1024)S(1)}, s32[49152]{0:T(1024)}, u32[]{:S(2)}) copy-start(s32[49152]{0:T(1024)} %param.10) | copy-start | bytes 589828
  67.7 38.5 %all-to-all-start = ((bf16[8,2,24576]{2,1,0:T(2,128)(2,1)}), bf16[8,2,24576]{2,1,0:T(2,128)(2,1)S(1)}, u32[]{:S(2)}, u32[]{:S(2)}) async-start(bf16[8,2,24576]{2,1,0:T(2,128)(2,1)} %reshape.54), calls=%async_computation | async-start | bytes 1572864 | tf_op jit(solution)/shard_map/all_to_all | solution.py:68
  75.8 19.3 %collective-permute-start = (bf16[2,384,128]{2,1,0:T(8,128)(2,1)S(1)}, bf16[2,384,128]{2,1,0:T(8,128)(2,1)S(1)}, u32[]{:S(2)}, u32[]{:S(2)}) collective-permute-start(bf16[2,384,128]{2,1,0:T(8,128)(2,1)S(1)} %bitcast.79), channel_id=1, source_target_pairs={{0,16},{16,32},{32,48},{48,64},{64,80},{80,96},{96,112},{112,0},{1... | collective-permute-start | bytes 589832 | tf_op jit(solution)/shard_map/ppermute | solution.py:13
  78.0 21.8 %collective-permute-start.2 = (bf16[2,384,128]{2,1,0:T(8,128)(2,1)S(1)}, bf16[2,384,128]{2,1,0:T(8,128)(2,1)S(1)}, u32[]{:S(2)}, u32[]{:S(2)}) collective-permute-start(bf16[2,384,128]{2,1,0:T(8,128)(2,1)S(1)} %bitcast.80), channel_id=1, source_target_pairs={{0,1},{1,2},{2,3},{3,4},{4,5},{5,6},{6,7},{7,8},{8,9},{9,10},{10,1... | collective-permute-start | bytes 589832 | tf_op jit(solution)/shard_map/ppermute | solution.py:13
  95.1 10.2 %collective-permute-start.1 = (bf16[2,384,128]{2,1,0:T(8,128)(2,1)S(1)}, bf16[2,384,128]{2,1,0:T(8,128)(2,1)S(1)}, u32[]{:S(2)}, u32[]{:S(2)}) collective-permute-start(bf16[2,384,128]{2,1,0:T(8,128)(2,1)S(1)} %collective-permute-done), channel_id=1, source_target_pairs={{0,16},{16,32},{32,48},{48,64},{64,80},{80,96},{96,112},{112,0},{1... | collective-permute-start | bytes 589832 | tf_op jit(solution)/shard_map/ppermute | solution.py:13
where the time goes:
time: 206 us; the launch traced here: 205 us
  local copies, waits for them, and re-layouts  55.1 us (27%)
  other arithmetic  51.6 us (25%)
  blocking collectives  23.4 us (11%)
  starting transfers between devices  22.1 us (11%)
  waiting for transfers between devices  19.1 us (9%)
  matrix products  18.7 us (9%)
  loops' own time  13.7 us (7%)
    unnamed x1, other arithmetic  45.2 us
    all_to_all x1, blocking collectives, per_device(): lax.all_to_all(rows_out, 'head', split_axis=0, concat_axis=1, tiled=True)  23.4 us
    ppermute x3, waiting for transfers between devices, passed_along(): lax.ppermute(value, axis, [(i, (i + by) % devices) for i in range(devices)])  19.1 us
    dot_general x8, matrix products, one_head(): lax.dot_general(query_now, key_now, (((1,), (1,)), ((), ())), preferred_e...  14.2 us
    another operation x1, loops' own time, attend_window(): lax.map(one_head, jnp.arange(query_head_stack.shape[0], dtype=jnp.int32))  13.7 us
    unnamed x14, local copies, waits for them, and re-layouts  13.5 us
    dynamic_update_slice x8, local copies, waits for them, and re-layouts, attend_window(): lax.map(one_head, jnp.arange(query_head_stack.shape[0], dtype=jnp.int32))  10.6 us
    dynamic_slice x8, local copies, waits for them, and re-layouts, attend_window(): lax.map(one_head, jnp.arange(query_head_stack.shape[0], dtype=jnp.int32))  10.1 us
  transfers between devices with their start and end apart: 5, of which 2 were waited for; matrix products, arithmetic and copies ran while one was open for 30% of the time, Pallas kernels for 0%

commit v1 on v0

v1 whole, which is shorter than its diff:
```python
import functools

import jax
import jax.numpy as jnp
from jax import lax
from jax.experimental import pallas as pl
from jax.experimental.pallas import tpu as pltpu
from jax.sharding import PartitionSpec as P

WIDTH = 128
GROUP = 8
STEPS = 4
LANES = 128
CHUNK_HEADS = 2
EARLY_CHUNKS = 2
QUERY_TILE = 128
MASKED = -1e30
MESH = pl.DeviceIdType.MESH


def attention_kernel(
    sizes,
    q_ref,
    k_ref,
    v_ref,
    place_ref,
    plan_ref,
    out_ref,
    log_ref,
    keys,
    values,
    q_buf,
    o_buf,
    bias,
    logs,
    place,
    plan,
    local_sem,
    kv_send,
    kv_recv,
    next_send,
    next_recv,
    q_send,
    q_recv,
    o_send,
    o_recv,
):
    heads, inners, outers = sizes
    rows = q_ref.shape[0]
    block_rows = rows * heads
    run = block_rows // 2
    chunks = GROUP // CHUNK_HEADS
    wide = CHUNK_HEADS * WIDTH
    me = lax.axis_index("head")
    inner = lax.axis_index("inner")
    outer = lax.axis_index("outer")
    offsets = sorted(range(1, heads), key=lambda r: -min(r, heads - r))

    def peer(r):
        return lax.rem(me + r, heads)

    def row_span(owner):
        return pl.ds(pl.multiple_of(owner * rows, 16), rows)

    targets = (
        {"inner": lax.rem(inner + 1, inners)},
        {"inner": lax.rem(inner + 2, inners)},
        {"outer": lax.rem(outer + 1, outers)},
    )
    origins = (
        {"inner": lax.rem(inner + inners - 1, inners)},
        {"inner": lax.rem(inner + inners - 2, inners)},
        {"outer": lax.rem(outer + outers - 1, outers)},
    )

    def kv_copy(which, r):
        ref, buf = ((k_ref, keys), (v_ref, values))[which]
        to = peer(r)
        return pltpu.make_async_remote_copy(
            src_ref=ref.at[:, pl.ds(pl.multiple_of(to * WIDTH, WIDTH), WIDTH)],
            dst_ref=buf.at[0, row_span(me), pl.ds(0, WIDTH)],
            send_sem=kv_send.at[which, r],
            recv_sem=kv_recv.at[which, r],
            device_id={"head": to},
            device_id_type=MESH,
        )

    def kv_landing(which, r):
        buf = (keys, values)[which]
        part = buf.at[0, row_span(lax.rem(me + heads - r, heads)), pl.ds(0, WIDTH)]
        return pltpu.make_async_remote_copy(
            src_ref=part,
            dst_ref=part,
            send_sem=kv_send.at[which, r],
            recv_sem=kv_recv.at[which, r],
            device_id={"head": peer(r)},
            device_id_type=MESH,
        )

    def next_copy(which, step):
        buf = (keys, values)[which]
        return pltpu.make_async_remote_copy(
            src_ref=buf.at[0, :, pl.ds(0, WIDTH)],
            dst_ref=buf.at[step + 1, :, pl.ds(0, WIDTH)],
            send_sem=next_send.at[which, step],
            recv_sem=next_recv.at[which, step],
            device_id=targets[step],
            device_id_type=MESH,
        )

    def q_columns(owner, c):
        return pl.ds(pl.multiple_of(owner * (GROUP * WIDTH) + c * wide, WIDTH), wide)

    def q_copy(c, r):
        to = peer(r)
        return pltpu.make_async_remote_copy(
            src_ref=q_ref.at[:, q_columns(to, c)],
            dst_ref=q_buf.at[c, row_span(me)],
            send_sem=q_send.at[c, r],
            recv_sem=q_recv.at[c, r],
            device_id={"head": to},
            device_id_type=MESH,
        )

    def q_landing(c, r):
        part = q_buf.at[c, row_span(lax.rem(me + heads - r, heads))]
        return pltpu.make_async_remote_copy(
            src_ref=part,
            dst_ref=part,
            send_sem=q_send.at[c, r],
            recv_sem=q_recv.at[c, r],
            device_id={"head": peer(r)},
            device_id_type=MESH,
        )

    def o_copy(c, r):
        to = peer(r)
        return pltpu.make_async_remote_copy(
            src_ref=o_buf.at[c, row_span(to)],
            dst_ref=out_ref.at[:, q_columns(me, c)],
            send_sem=o_send.at[c, r],
            recv_sem=o_recv.at[c, r],
            device_id={"head": to},
            device_id_type=MESH,
        )

    def o_landing(c, r):
        part = out_ref.at[:, q_columns(lax.rem(me + heads - r, heads), c)]
        return pltpu.make_async_remote_copy(
            src_ref=part,
            dst_ref=part,
            send_sem=o_send.at[c, r],
            recv_sem=o_recv.at[c, r],
            device_id={"head": peer(r)},
            device_id_type=MESH,
        )

    own_kv = [
        pltpu.make_async_copy(
            ref.at[:, pl.ds(pl.multiple_of(me * WIDTH, WIDTH), WIDTH)],
            buf.at[0, row_span(me), pl.ds(0, WIDTH)],
            local_sem.at[n],
        )
        for n, (ref, buf) in enumerate(((k_ref, keys), (v_ref, values)))
    ]
    tables = [
        pltpu.make_async_copy(place_ref, place, local_sem.at[2]),
        pltpu.make_async_copy(plan_ref, plan, local_sem.at[3]),
    ]

    def own_q(c):
        return pltpu.make_async_copy(
            q_ref.at[:, q_columns(me, c)], q_buf.at[c, row_span(me)], q_send.at[c, 0]
        )

    def own_o(c):
        return pltpu.make_async_copy(
            o_buf.at[c, row_span(me)], out_ref.at[:, q_columns(me, c)], o_send.at[c, 0]
        )

    barrier = pltpu.get_barrier_semaphore()
    for r in offsets:
        pl.semaphore_signal(barrier, inc=1, device_id={"head": peer(r)}, device_id_type=MESH)
    for origin in origins:
        pl.semaphore_signal(barrier, inc=1, device_id=origin, device_id_type=MESH)
    for copy in own_kv + tables:
        copy.start()
    for c in range(chunks):
        own_q(c).start()
    pl.semaphore_wait(barrier, len(offsets) + len(origins))

    for r in offsets:
        kv_copy(0, r).start()
        kv_copy(1, r).start()
    for c in range(EARLY_CHUNKS):
        for r in offsets:
            q_copy(c, r).start()

    for copy in tables:
        copy.wait()
    here = inner * outers + outer
    sources = (
        here,
        lax.rem(inner + inners - 1, inners) * outers + outer,
        lax.rem(inner + inners - 2, inners) * outers + outer,
        inner * outers + lax.rem(outer + outers - 1, outers),
    )
    def starts(block):
        first = block * block_rows
        second = first + run
        out = []
        for spot in (first, second):
            line = place[pl.ds(lax.div(spot, LANES), 1), :]
            lane = lax.broadcasted_iota(jnp.int32, (1, LANES), 1)
            out.append(
                jnp.sum(
                    jnp.where(lane == lax.rem(spot, LANES), line, 0), axis=1, keepdims=True
                )
            )
        return out

    lane = lax.broadcasted_iota(jnp.int32, plan.shape, 1)
    used = jnp.max(jnp.where(lane == here, plan[...], 0), axis=1, keepdims=True)
    q_first, q_second = starts(here)
    q_row = lax.broadcasted_iota(jnp.int32, (block_rows, 1), 0)
    q_place = jnp.where(q_row < run, q_first + q_row, q_second + q_row - run)
    k_row = lax.broadcasted_iota(jnp.int32, (1, block_rows), 1)
    for step, source in enumerate(sources):
        k_first, k_second = starts(source)
        k_place = jnp.where(k_row < run, k_first + k_row, k_second + k_row - run)
        if step:
            k_place = jnp.where(used[step - 1 : step] == 1, k_place, jnp.int32(2**30))
        bias[:, step * block_rows : (step + 1) * block_rows] = jnp.where(
            k_place <= q_place, jnp.float32(0), jnp.float32(MASKED)
        )
    values[:, :, WIDTH:] = jnp.ones((STEPS, block_rows, LANES), values.dtype)
    logs[...] = jnp.zeros_like(logs)

    for which in range(2):
        own_kv[which].wait()
        for r in offsets:
            kv_landing(which, r).wait_recv()
        for step in range(STEPS - 1):
            next_copy(which, step).start()
    for c in range(EARLY_CHUNKS, chunks):
        for r in offsets:
            q_copy(c, r).start()
    for which in range(2):
        for step in range(STEPS - 1):
            next_copy(which, step).wait_recv()

    scale = WIDTH**-0.5
    exponent = scale * 1.4426950408889634

    def one_chunk(c, carry):
        own_q(c).wait()
        for r in offsets:
            q_landing(c, r).wait_recv()
        for j in range(CHUNK_HEADS):
            columns = slice(j * WIDTH, (j + 1) * WIDTH)
            for tile in range(0, block_rows, QUERY_TILE):
                span = slice(tile, tile + QUERY_TILE)
                query = q_buf[c, span, columns]
                scores = [
                    lax.dot_general(
                        query,
                        keys[step],
                        (((1,), (1,)), ((), ())),
                        preferred_element_type=jnp.float32,
                    )
                    + bias[span, step * block_rows : (step + 1) * block_rows]
                    for step in range(STEPS)
                ]
                top = functools.reduce(jnp.maximum, scores)
                top = jnp.max(top, axis=1, keepdims=True)
                mixed = jnp.zeros((QUERY_TILE, 2 * WIDTH), jnp.float32)
                for step in range(STEPS):
                    weights = jnp.exp2((scores[step] - top) * exponent)
                    mixed += jnp.dot(
                        weights.astype(jnp.bfloat16),
                        values[step],
                        preferred_element_type=jnp.float32,
                    )
                total = mixed[:, WIDTH:]
                o_buf[c, span, columns] = (mixed[:, :WIDTH] / total).astype(o_buf.dtype)
                lane = lax.broadcasted_iota(jnp.int32, (QUERY_TILE, LANES), 1)
                logs[span, :] = jnp.where(
                    lane == c * CHUNK_HEADS + j, top * scale + jnp.log(total), logs[span, :]
                )
        own_o(c).start()
        for r in offsets:
            o_copy(c, r).start()
        return carry

    lax.fori_loop(0, chunks, one_chunk, 0)
    log_ref[...] = jnp.transpose(logs[...])[:GROUP]

    for which in range(2):
        for r in offsets:
            kv_copy(which, r).wait_send()
        for step in range(STEPS - 1):
            next_copy(which, step).wait_send()
    for c in range(chunks):
        own_o(c).wait()
        for r in offsets:
            q_copy(c, r).wait_send()
            o_copy(c, r).wait_send()
            o_landing(c, r).wait_recv()


def per_device(queries, keys, values, positions, plan):
    sizes = tuple(lax.axis_size(name) for name in ("head", "inner", "outer"))
    heads = sizes[0]
    rows = queries.shape[0]
    block_rows = rows * heads
    chunks = GROUP // CHUNK_HEADS
    place = positions.reshape(-1, LANES)
    used = plan.T
    anywhere = pl.BlockSpec(memory_space=pl.ANY)
    dma = pltpu.SemaphoreType.DMA
    kind = queries.dtype
    return pl.pallas_call(
        functools.partial(attention_kernel, sizes),
        out_shape=(
            jax.ShapeDtypeStruct(queries.shape, kind),
            jax.ShapeDtypeStruct((GROUP, block_rows), jnp.float32),
        ),
        in_specs=[anywhere] * 5,
        out_specs=(anywhere, pl.BlockSpec(memory_space=pltpu.VMEM)),
        scratch_shapes=[
            pltpu.VMEM((STEPS, block_rows, WIDTH), kind),
            pltpu.VMEM((STEPS, block_rows, 2 * WIDTH), kind),
            pltpu.VMEM((chunks, block_rows, CHUNK_HEADS * WIDTH), kind),
            pltpu.VMEM((chunks, block_rows, CHUNK_HEADS * WIDTH), kind),
            pltpu.VMEM((block_rows, STEPS * block_rows), jnp.float32),
            pltpu.VMEM((block_rows, LANES), jnp.float32),
            pltpu.VMEM(place.shape, jnp.int32),
            pltpu.VMEM(used.shape, jnp.int32),
            dma((4,)),
            dma((2, heads)),
            dma((2, heads)),
            dma((2, STEPS - 1)),
            dma((2, STEPS - 1)),
            dma((chunks, heads)),
            dma((chunks, heads)),
            dma((chunks, heads)),
            dma((chunks, heads)),
        ],
        compiler_params=pltpu.CompilerParams(
            collective_id=0, has_side_effects=True, vmem_limit_bytes=40 * 1024 * 1024
        ),
    )(queries, keys, values, place, used)


def solution(mesh):
    rows = P(("inner", "outer", "head"), None)
    return jax.shard_map(
        per_device,
        mesh=mesh,
        in_specs=(rows, rows, rows, P(), P()),
        out_specs=(rows, P("head", ("inner", "outer"))),
        check_vma=False,
    )
```

time: 206 us -> 74.3 us (0.36)
  the two profiles are of different devices: /device:TPU:128 before, /device:TPU:1 now
where the time goes in v1:
time: 74.3 us; the launch traced here: 74 us
  Pallas kernels  67.4 us (91%)
  local copies, waits for them, and re-layouts  6 us (8%)
    pallas_call x1, Pallas kernels, per_device(): pl.pallas_call(functools.partial(attention_kernel, sizes), out_shape=(jax...  67.4 us
    unnamed x12, local copies, waits for them, and re-layouts  6 us

profile of v1, /device:TPU:1, one launch (start us, length us, event | category | flops | bytes accessed | tf_op | source)
XLA Modules:
  0.0 74.0 jit_solution(8884770327133711326)
XLA Ops:
  0.6 0.0 copy-start.4
  0.6 0.7 copy-done.4
  1.3 0.0 copy-start
  1.3 1.1 %copy-done = bf16[48,8192]{1,0:T(8,128)(2,1)S(1)} copy-done((bf16[48,8192]{1,0:T(8,128)(2,1)S(1)}, bf16[48,8192]{1,0:T(8,128)(2,1)}, u32[]{:S(2)}) %copy-start) | copy-done | bytes 786456
  2.4 0.0 copy-start.1
  2.4 0.9 %copy-done.1 = s32[49152]{0:T(1024)S(1)} copy-done((s32[49152]{0:T(1024)S(1)}, s32[49152]{0:T(1024)}, u32[]{:S(2)}) %copy-start.1) | copy-done | bytes 196632
  3.4 0.0 copy-start.2
  3.4 0.9 %copy-done.2 = bf16[48,1024]{1,0:T(8,128)(2,1)S(1)} copy-done((bf16[48,1024]{1,0:T(8,128)(2,1)S(1)}, bf16[48,1024]{1,0:T(8,128)(2,1)}, u32[]{:S(2)}) %copy-start.2) | copy-done | bytes 98328
  4.3 0.0 copy-start.3
  4.3 0.9 %copy-done.3 = bf16[48,1024]{1,0:T(8,128)(2,1)S(1)} copy-done((bf16[48,1024]{1,0:T(8,128)(2,1)S(1)}, bf16[48,1024]{1,0:T(8,128)(2,1)}, u32[]{:S(2)}) %copy-start.3) | copy-done | bytes 98328
  5.2 67.4 %shard_map.68 = (bf16[48,8192]{1,0:T(8,128)(2,1)S(1)}, f32[8,384]{1,0:T(8,128)S(1)}) custom-call(bf16[48,8192]{1,0:T(8,128)(2,1)S(1)} %copy-done, bf16[48,1024]{1,0:T(8,128)(2,1)S(1)} %copy-done.2, bf16[48,1024]{1,0:T(8,128)(2,1)S(1)} %copy-done.3, s32[384,128]{1,0:T(8,128)S(1)} %bitcast.2, s32[3,128]{1,0:T(4,128)S(1)} %bitcast.3), custom_call_target="tpu_custom_call" | custom-call | tf_op jit(solution)/shard_map/pallas_call | solution.py:322
  72.5 0.9 %copy.9 = bf16[48,8192]{1,0:T(8,128)(2,1)} copy(bf16[48,8192]{1,0:T(8,128)(2,1)S(1)} %get-tuple-element.4) | data formatting | bytes 1572864
  73.4 0.6 copy.10
Async XLA Ops:
  0.6 0.7 copy-start.4
  1.3 1.1 %copy-start = (bf16[48,8192]{1,0:T(8,128)(2,1)S(1)}, bf16[48,8192]{1,0:T(8,128)(2,1)}, u32[]{:S(2)}) copy-start(bf16[48,8192]{1,0:T(8,128)(2,1)} %q_ref.1) | copy-start | bytes 2359300
  2.4 0.9 %copy-start.1 = (s32[49152]{0:T(1024)S(1)}, s32[49152]{0:T(1024)}, u32[]{:S(2)}) copy-start(s32[49152]{0:T(1024)} %param.8) | copy-start | bytes 589828
  3.4 0.9 %copy-start.2 = (bf16[48,1024]{1,0:T(8,128)(2,1)S(1)}, bf16[48,1024]{1,0:T(8,128)(2,1)}, u32[]{:S(2)}) copy-start(bf16[48,1024]{1,0:T(8,128)(2,1)} %k_ref.1) | copy-start | bytes 294916
  4.3 0.9 %copy-start.3 = (bf16[48,1024]{1,0:T(8,128)(2,1)S(1)}, bf16[48,1024]{1,0:T(8,128)(2,1)}, u32[]{:S(2)}) copy-start(bf16[48,1024]{1,0:T(8,128)(2,1)} %v_ref.1) | copy-start | bytes 294916

commit v2 on v1

--- a/solution.py
+++ b/solution.py
@@ -12,9 +12,10 @@
 STEPS = 4
 LANES = 128
 CHUNK_HEADS = 2
-EARLY_CHUNKS = 2
-QUERY_TILE = 128
+EARLY_CHUNKS = 1
+QUERY_TILE = 192
 MASKED = -1e30
+HAND_OVER_PARTS = 3
 MESH = pl.DeviceIdType.MESH
 
 
@@ -27,8 +28,7 @@
     plan_ref,
     out_ref,
     log_ref,
-    keys,
-    values,
+    kv_buf,
     q_buf,
     o_buf,
     bias,
@@ -40,6 +40,7 @@
     kv_recv,
     next_send,
     next_recv,
+    relay_send,
     q_send,
     q_recv,
     o_send,
@@ -55,6 +56,9 @@
     inner = lax.axis_index("inner")
     outer = lax.axis_index("outer")
     offsets = sorted(range(1, heads), key=lambda r: -min(r, heads - r))
+    pieces = [0] + offsets[::-1]
+    side = lax.rem(inner, 2)
+    even = side == 0
 
     def peer(r):
         return lax.rem(me + r, heads)
@@ -73,21 +77,26 @@
         {"outer": lax.rem(outer + outers - 1, outers)},
     )
 
+    partner = {"inner": inner + 1 - 2 * side}
+    key_value = pl.ds(0, WIDTH)
+
     def kv_copy(which, r):
-        ref, buf = ((k_ref, keys), (v_ref, values))[which]
+        ref = (k_ref, v_ref)[which]
         to = peer(r)
         return pltpu.make_async_remote_copy(
             src_ref=ref.at[:, pl.ds(pl.multiple_of(to * WIDTH, WIDTH), WIDTH)],
-            dst_ref=buf.at[0, row_span(me), pl.ds(0, WIDTH)],
+            dst_ref=kv_buf.at[which, 0, row_span(me), key_value],
             send_sem=kv_send.at[which, r],
             recv_sem=kv_recv.at[which, r],
             device_id={"head": to},
             device_id_type=MESH,
         )
 
+    def piece(which, slot, r):
+        return kv_buf.at[which, slot, row_span(lax.rem(me + heads - r, heads)), key_value]
+
     def kv_landing(which, r):
-        buf = (keys, values)[which]
-        part = buf.at[0, row_span(lax.rem(me + heads - r, heads)), pl.ds(0, WIDTH)]
+        part = piece(which, 0, r)
         return pltpu.make_async_remote_copy(
             src_ref=part,
             dst_ref=part,
@@ -97,14 +106,42 @@
             device_id_type=MESH,
         )
 
-    def next_copy(which, step):
-        buf = (keys, values)[which]
-        return pltpu.make_async_remote_copy(
-            src_ref=buf.at[0, :, pl.ds(0, WIDTH)],
-            dst_ref=buf.at[step + 1, :, pl.ds(0, WIDTH)],
-            send_sem=next_send.at[which, step],
-            recv_sem=next_recv.at[which, step],
+    def next_copy(which, step, r):
+        return pltpu.make_async_remote_copy(
+            src_ref=piece(which, 0, r),
+            dst_ref=piece(which, step + 1, r),
+            send_sem=next_send.at[which, step, r],
+            recv_sem=next_recv.at[which, step, r],
             device_id=targets[step],
+            device_id_type=MESH,
+        )
+
+    def next_copies(which, r, act):
+        act(next_copy(which, 2, r))
+        act(next_copy(which, which, r))
+
+        @pl.when(even)
+        def _():
+            act(next_copy(which, 1 - which, r))
+
+    def relay_copy(r):
+        return pltpu.make_async_remote_copy(
+            src_ref=piece(side, 1 + side, r),
+            dst_ref=piece(side, 2 - side, r),
+            send_sem=relay_send.at[r],
+            recv_sem=next_recv.at[side, 1 - side, r],
+            device_id=partner,
+            device_id_type=MESH,
+        )
+
+    def next_landing(which, step, r):
+        part = piece(which, step + 1, r)
+        return pltpu.make_async_remote_copy(
+            src_ref=part,
+            dst_ref=part,
+            send_sem=relay_send.at[r],
+            recv_sem=next_recv.at[which, step, r],
+            device_id=partner,
             device_id_type=MESH,
         )
 
@@ -158,10 +195,10 @@
     own_kv = [
         pltpu.make_async_copy(
             ref.at[:, pl.ds(pl.multiple_of(me * WIDTH, WIDTH), WIDTH)],
-            buf.at[0, row_span(me), pl.ds(0, WIDTH)],
+            kv_buf.at[n, 0, row_span(me), key_value],
             local_sem.at[n],
         )
-        for n, (ref, buf) in enumerate(((k_ref, keys), (v_ref, values)))
+        for n, ref in enumerate((k_ref, v_ref))
     ]
     tables = [
         pltpu.make_async_copy(place_ref, place, local_sem.at[2]),
@@ -189,7 +226,7 @@
         own_q(c).start()
     pl.semaphore_wait(barrier, len(offsets) + len(origins))
 
-    for r in offsets:
+    for r in offsets[::-1]:
         kv_copy(0, r).start()
         kv_copy(1, r).start()
     for c in range(EARLY_CHUNKS):
@@ -233,21 +270,36 @@
         bias[:, step * block_rows : (step + 1) * block_rows] = jnp.where(
             k_place <= q_place, jnp.float32(0), jnp.float32(MASKED)
         )
-    values[:, :, WIDTH:] = jnp.ones((STEPS, block_rows, LANES), values.dtype)
+    kv_buf[1, :, :, WIDTH:] = jnp.ones((STEPS, block_rows, LANES), kv_buf.dtype)
     logs[...] = jnp.zeros_like(logs)
 
-    for which in range(2):
-        own_kv[which].wait()
-        for r in offsets:
-            kv_landing(which, r).wait_recv()
-        for step in range(STEPS - 1):
-            next_copy(which, step).start()
+    for r in pieces:
+        for which in range(2):
+            if r:
+                kv_landing(which, r).wait_recv()
+            else:
+                own_kv[which].wait()
+            next_copies(which, r, lambda copy: copy.start())
     for c in range(EARLY_CHUNKS, chunks):
         for r in offsets:
             q_copy(c, r).start()
-    for which in range(2):
-        for step in range(STEPS - 1):
-            next_copy(which, step).wait_recv()
+
+    @pl.when(jnp.logical_not(even))
+    def _():
+        next_landing(0, 0, 0).wait_recv()
+
+    for r in pieces:
+        next_landing(side, side, r).wait_recv()
+        relay_copy(r).start()
+    for r in pieces:
+        for which, step in ((1 - side, 1), (0, 2), (1, 2), (side, 1 - side)):
+            next_landing(which, step, r).wait_recv()
+        if r:
+            next_landing(1 - side, 0, r).wait_recv()
+
+    @pl.when(even)
+    def _():
+        next_landing(1, 0, 0).wait_recv()
 
     scale = WIDTH**-0.5
     exponent = scale * 1.4426950408889634
@@ -264,7 +316,7 @@
                 scores = [
                     lax.dot_general(
                         query,
-                        keys[step],
+                        kv_buf[0, step, :, :WIDTH],
                         (((1,), (1,)), ((), ())),
                         preferred_element_type=jnp.float32,
                     )
@@ -278,7 +330,7 @@
                     weights = jnp.exp2((scores[step] - top) * exponent)
                     mixed += jnp.dot(
                         weights.astype(jnp.bfloat16),
-                        values[step],
+                        kv_buf[1, step],
                         preferred_element_type=jnp.float32,
                     )
                 total = mixed[:, WIDTH:]
@@ -295,17 +347,40 @@
     lax.fori_loop(0, chunks, one_chunk, 0)
     log_ref[...] = jnp.transpose(logs[...])[:GROUP]
 
-    for which in range(2):
-        for r in offsets:
-            kv_copy(which, r).wait_send()
-        for step in range(STEPS - 1):
-            next_copy(which, step).wait_send()
+    for r in pieces:
+        for which in range(2):
+            if r:
+                kv_copy(which, r).wait_send()
+            next_copies(which, r, lambda copy: copy.wait_send())
+        relay_copy(r).wait_send()
     for c in range(chunks):
         own_o(c).wait()
         for r in offsets:
             q_copy(c, r).wait_send()
             o_copy(c, r).wait_send()
             o_landing(c, r).wait_recv()
+
+
+def hand_over(mixed_ref, log_in_ref, out_ref, log_ref, mixed, log, in_sem, out_sem):
+    part = mixed_ref.shape[0] // HAND_OVER_PARTS
+    spans = [pl.ds(n * part, part) for n in range(HAND_OVER_PARTS)]
+    pairs = [(log_in_ref, log, log_ref)] + [
+        (mixed_ref.at[span], mixed.at[span], out_ref.at[span]) for span in spans
+    ]
+    copies = [
+        (
+            pltpu.make_async_copy(source, stop, in_sem.at[n]),
+            pltpu.make_async_copy(stop, end, out_sem.at[n]),
+        )
+        for n, (source, stop, end) in enumerate(pairs)
+    ]
+    for load, _ in copies:
+        load.start()
+    for load, store in copies:
+        load.wait()
+        store.start()
+    for _, store in copies:
+        store.wait()
 
 
 def per_device(queries, keys, values, positions, plan):
@@ -319,7 +394,7 @@
     anywhere = pl.BlockSpec(memory_space=pl.ANY)
     dma = pltpu.SemaphoreType.DMA
     kind = queries.dtype
-    return pl.pallas_call(
+    results = pl.pallas_call(
         functools.partial(attention_kernel, sizes),
         out_shape=(
             jax.ShapeDtypeStruct(queries.shape, kind),
@@ -328,8 +403,7 @@
         in_specs=[anywhere] * 5,
         out_specs=(anywhere, pl.BlockSpec(memory_space=pltpu.VMEM)),
         scratch_shapes=[
-            pltpu.VMEM((STEPS, block_rows, WIDTH), kind),
-            pltpu.VMEM((STEPS, block_rows, 2 * WIDTH), kind),
+            pltpu.VMEM((2, STEPS, block_rows, 2 * WIDTH), kind),
             pltpu.VMEM((chunks, block_rows, CHUNK_HEADS * WIDTH), kind),
             pltpu.VMEM((chunks, block_rows, CHUNK_HEADS * WIDTH), kind),
             pltpu.VMEM((block_rows, STEPS * block_rows), jnp.float32),
@@ -339,17 +413,30 @@
             dma((4,)),
             dma((2, heads)),
             dma((2, heads)),
-            dma((2, STEPS - 1)),
-            dma((2, STEPS - 1)),
+            dma((2, STEPS - 1, heads)),
+            dma((2, STEPS - 1, heads)),
+            dma((heads,)),
             dma((chunks, heads)),
             dma((chunks, heads)),
             dma((chunks, heads)),
             dma((chunks, heads)),
         ],
         compiler_params=pltpu.CompilerParams(
-            collective_id=0, has_side_effects=True, vmem_limit_bytes=40 * 1024 * 1024
+            collective_id=0, has_side_effects=True, vmem_limit_bytes=58 * 1024 * 1024
         ),
     )(queries, keys, values, place, used)
+    return pl.pallas_call(
+        hand_over,
+        out_shape=tuple(jax.ShapeDtypeStruct(x.shape, x.dtype) for x in results),
+        in_specs=[anywhere] * 2,
+        out_specs=(anywhere,) * 2,
+        scratch_shapes=[
+            *(pltpu.VMEM(x.shape, x.dtype) for x in results),
+            dma((HAND_OVER_PARTS + 1,)),
+            dma((HAND_OVER_PARTS + 1,)),
+        ],
+        compiler_params=pltpu.CompilerParams(vmem_limit_bytes=58 * 1024 * 1024),
+    )(*results)
 
 
 def solution(mesh):

time: 74.3 us -> 64.4 us (0.87)
  local copies, waits for them, and re-layouts: 6 us -> 0 us
  Pallas kernels: 67.4 us -> 63.5 us
    unnamed x12 -> x0, local copies, waits for them, and re-layouts: 6 us -> none
    pallas_call x1, Pallas kernels: 67.4 us -> 61.6 us  [per_device(): pl.pallas_call(functools.partial(attention_kernel, sizes), out_shape=(jax...]
    pallas_call x0 -> x1, Pallas kernels: none -> 1.91 us  [per_device(): pl.pallas_call(hand_over, out_shape=tuple((jax.ShapeDtypeStruct(x.shape,...]
where the time goes in v2:
time: 64.4 us; the launch traced here: 64.2 us
  Pallas kernels  63.5 us (99%)
    pallas_call x1, Pallas kernels, per_device(): pl.pallas_call(functools.partial(attention_kernel, sizes), out_shape=(jax...  61.6 us
    pallas_call x1, Pallas kernels, per_device(): pl.pallas_call(hand_over, out_shape=tuple((jax.ShapeDtypeStruct(x.shape,...  1.91 us

profile of v2, /device:TPU:1, one launch (start us, length us, event | category | flops | bytes accessed | tf_op | source)
XLA Modules:
  0.0 64.2 jit_solution(16706557224495944831)
XLA Ops:
  0.6 61.6 %shard_map.68 = (bf16[48,8192]{1,0:T(8,128)(2,1)}, f32[8,384]{1,0:T(8,128)}) custom-call(bf16[48,8192]{1,0:T(8,128)(2,1)} %q_ref.1, bf16[48,1024]{1,0:T(8,128)(2,1)} %k_ref.1, bf16[48,1024]{1,0:T(8,128)(2,1)} %v_ref.1, s32[384,128]{1,0:T(8,128)} %bitcast.2, s32[3,128]{1,0:T(4,128)} %bitcast.3), custom_call_target="tpu_custom_call" | custom-call | tf_op jit(solution)/shard_map/pallas_call | solution.py:397
  62.3 1.9 %shard_map.69 = (bf16[48,8192]{1,0:T(8,128)(2,1)}, f32[8,384]{1,0:T(8,128)}) custom-call(bf16[48,8192]{1,0:T(8,128)(2,1)} %get-tuple-element.4.mixed_ref, f32[8,384]{1,0:T(8,128)} %get-tuple-element.5.log_in_ref), custom_call_target="tpu_custom_call" | custom-call | tf_op jit(solution)/shard_map/pallas_call | solution.py:428

commit v3 on v2

--- a/solution.py
+++ b/solution.py
@@ -41,6 +41,7 @@
     next_send,
     next_recv,
     relay_send,
+    relay_recv,
     q_send,
     q_recv,
     o_send,
@@ -86,8 +87,8 @@
         return pltpu.make_async_remote_copy(
             src_ref=ref.at[:, pl.ds(pl.multiple_of(to * WIDTH, WIDTH), WIDTH)],
             dst_ref=kv_buf.at[which, 0, row_span(me), key_value],
-            send_sem=kv_send.at[which, r],
-            recv_sem=kv_recv.at[which, r],
+            send_sem=kv_send.at[r],
+            recv_sem=kv_recv.at[r],
             device_id={"head": to},
             device_id_type=MESH,
         )
@@ -95,55 +96,65 @@
     def piece(which, slot, r):
         return kv_buf.at[which, slot, row_span(lax.rem(me + heads - r, heads)), key_value]
 
-    def kv_landing(which, r):
-        part = piece(which, 0, r)
+    both = slice(None)
+
+    def arrival(part, send_sem, recv_sem):
         return pltpu.make_async_remote_copy(
             src_ref=part,
             dst_ref=part,
-            send_sem=kv_send.at[which, r],
-            recv_sem=kv_recv.at[which, r],
-            device_id={"head": peer(r)},
-            device_id_type=MESH,
-        )
+            send_sem=send_sem,
+            recv_sem=recv_sem,
+            device_id=partner,
+            device_id_type=MESH,
+        )
+
+    def kv_landing(r):
+        return arrival(piece(both, 0, r), kv_send.at[r], kv_recv.at[r])
 
     def next_copy(which, step, r):
         return pltpu.make_async_remote_copy(
             src_ref=piece(which, 0, r),
             dst_ref=piece(which, step + 1, r),
-            send_sem=next_send.at[which, step, r],
-            recv_sem=next_recv.at[which, step, r],
+            send_sem=next_send.at[step, r],
+            recv_sem=next_recv.at[step, r],
             device_id=targets[step],
             device_id_type=MESH,
         )
 
-    def next_copies(which, r, act):
-        act(next_copy(which, 2, r))
-        act(next_copy(which, which, r))
-
+    def next_copies(r, act):
         @pl.when(even)
         def _():
-            act(next_copy(which, 1 - which, r))
+            act(next_copy(both, 1, r))
+            act(next_copy(both, 0, r))
+
+        @pl.when(jnp.logical_not(even))
+        def _():
+            act(next_copy(0, 0, r))
+            act(next_copy(1, 1, r))
+
+        act(next_copy(both, 2, r))
+
+    def whole_landing(r):
+        return arrival(piece(both, 2 - side, r), relay_send.at[r], next_recv.at[1 - side, r])
+
+    def half_landing(r):
+        return arrival(piece(side, 1 + side, r), relay_send.at[r], next_recv.at[side, r])
+
+    def outer_landing(r):
+        return arrival(piece(both, 3, r), relay_send.at[r], next_recv.at[2, r])
 
     def relay_copy(r):
         return pltpu.make_async_remote_copy(
             src_ref=piece(side, 1 + side, r),
             dst_ref=piece(side, 2 - side, r),
             send_sem=relay_send.at[r],
-            recv_sem=next_recv.at[side, 1 - side, r],
+            recv_sem=relay_recv.at[r],
             device_id=partner,
             device_id_type=MESH,
         )
 
-    def next_landing(which, step, r):
-        part = piece(which, step + 1, r)
-        return pltpu.make_async_remote_copy(
-            src_ref=part,
-            dst_ref=part,
-            send_sem=relay_send.at[r],
-            recv_sem=next_recv.at[which, step, r],
-            device_id=partner,
-            device_id_type=MESH,
-        )
+    def relay_landing(r):
+        return arrival(piece(1 - side, 1 + side, r), relay_send.at[r], relay_recv.at[r])
 
     def q_columns(owner, c):
         return pl.ds(pl.multiple_of(owner * (GROUP * WIDTH) + c * wide, WIDTH), wide)
@@ -229,7 +240,17 @@
     for r in offsets[::-1]:
         kv_copy(0, r).start()
         kv_copy(1, r).start()
+
+    for copy in own_kv:
+        copy.wait()
+    next_copies(0, lambda copy: copy.start())
     for c in range(EARLY_CHUNKS):
+        for r in offsets:
+            q_copy(c, r).start()
+    for r in pieces[1:]:
+        kv_landing(r).wait_recv()
+        next_copies(r, lambda copy: copy.start())
+    for c in range(EARLY_CHUNKS, chunks):
         for r in offsets:
             q_copy(c, r).start()
 
@@ -273,33 +294,24 @@
     kv_buf[1, :, :, WIDTH:] = jnp.ones((STEPS, block_rows, LANES), kv_buf.dtype)
     logs[...] = jnp.zeros_like(logs)
 
-    for r in pieces:
-        for which in range(2):
-            if r:
-                kv_landing(which, r).wait_recv()
-            else:
-                own_kv[which].wait()
-            next_copies(which, r, lambda copy: copy.start())
-    for c in range(EARLY_CHUNKS, chunks):
-        for r in offsets:
-            q_copy(c, r).start()
-
     @pl.when(jnp.logical_not(even))
     def _():
-        next_landing(0, 0, 0).wait_recv()
+        whole_landing(0).wait_recv()
 
     for r in pieces:
-        next_landing(side, side, r).wait_recv()
+        half_landing(r).wait_recv()
         relay_copy(r).start()
     for r in pieces:
-        for which, step in ((1 - side, 1), (0, 2), (1, 2), (side, 1 - side)):
-            next_landing(which, step, r).wait_recv()
+        outer_landing(r).wait_recv()
         if r:
-            next_landing(1 - side, 0, r).wait_recv()
+            whole_landing(r).wait_recv()
 
     @pl.when(even)
     def _():
-        next_landing(1, 0, 0).wait_recv()
+        whole_landing(0).wait_recv()
+
+    for r in pieces:
+        relay_landing(r).wait_recv()
 
     scale = WIDTH**-0.5
     exponent = scale * 1.4426950408889634
@@ -348,10 +360,9 @@
     log_ref[...] = jnp.transpose(logs[...])[:GROUP]
 
     for r in pieces:
-        for which in range(2):
-            if r:
-                kv_copy(which, r).wait_send()
-            next_copies(which, r, lambda copy: copy.wait_send())
+        if r:
+            kv_landing(r).wait_send()
+        next_copies(r, lambda copy: copy.wait_send())
         relay_copy(r).wait_send()
     for c in range(chunks):
         own_o(c).wait()
@@ -361,26 +372,16 @@
             o_landing(c, r).wait_recv()
 
 
-def hand_over(mixed_ref, log_in_ref, out_ref, log_ref, mixed, log, in_sem, out_sem):
+def hand_over(mixed_ref, log_in_ref, out_ref, log_ref, sem):
     part = mixed_ref.shape[0] // HAND_OVER_PARTS
-    spans = [pl.ds(n * part, part) for n in range(HAND_OVER_PARTS)]
-    pairs = [(log_in_ref, log, log_ref)] + [
-        (mixed_ref.at[span], mixed.at[span], out_ref.at[span]) for span in spans
-    ]
-    copies = [
-        (
-            pltpu.make_async_copy(source, stop, in_sem.at[n]),
-            pltpu.make_async_copy(stop, end, out_sem.at[n]),
-        )
-        for n, (source, stop, end) in enumerate(pairs)
-    ]
-    for load, _ in copies:
-        load.start()
-    for load, store in copies:
-        load.wait()
-        store.start()
-    for _, store in copies:
-        store.wait()
+    copies = [pltpu.make_async_copy(log_in_ref, log_ref, sem.at[HAND_OVER_PARTS])]
+    for n in range(HAND_OVER_PARTS):
+        span = pl.ds(n * part, part)
+        copies.append(pltpu.make_async_copy(mixed_ref.at[span], out_ref.at[span], sem.at[n]))
+    for copy in copies:
+        copy.start()
+    for copy in copies:
+        copy.wait()
 
 
 def per_device(queries, keys, values, positions, plan):
@@ -394,6 +395,10 @@
     anywhere = pl.BlockSpec(memory_space=pl.ANY)
     dma = pltpu.SemaphoreType.DMA
     kind = queries.dtype
+    queries, keys, values, place, used = (
+        pltpu.with_memory_space_constraint(x, pltpu.HBM)
+        for x in (queries, keys, values, place, used)
+    )
     results = pl.pallas_call(
         functools.partial(attention_kernel, sizes),
         out_shape=(
@@ -411,10 +416,11 @@
             pltpu.VMEM(place.shape, jnp.int32),
             pltpu.VMEM(used.shape, jnp.int32),
             dma((4,)),
-            dma((2, heads)),
-            dma((2, heads)),
-            dma((2, STEPS - 1, heads)),
-            dma((2, STEPS - 1, heads)),
+            dma((heads,)),
+            dma((heads,)),
+            dma((STEPS - 1, heads)),
+            dma((STEPS - 1, heads)),
+            dma((heads,)),
             dma((heads,)),
             dma((chunks, heads)),
             dma((chunks, heads)),
@@ -422,7 +428,7 @@
             dma((chunks, heads)),
         ],
         compiler_params=pltpu.CompilerParams(
-            collective_id=0, has_side_effects=True, vmem_limit_bytes=58 * 1024 * 1024
+            collective_id=0, has_side_effects=True, vmem_limit_bytes=30 * 1024 * 1024
         ),
     )(queries, keys, values, place, used)
     return pl.pallas_call(
@@ -431,11 +437,9 @@
         in_specs=[anywhere] * 2,
         out_specs=(anywhere,) * 2,
         scratch_shapes=[
-            *(pltpu.VMEM(x.shape, x.dtype) for x in results),
-            dma((HAND_OVER_PARTS + 1,)),
             dma((HAND_OVER_PARTS + 1,)),
         ],
-        compiler_params=pltpu.CompilerParams(vmem_limit_bytes=58 * 1024 * 1024),
+        compiler_params=pltpu.CompilerParams(vmem_limit_bytes=30 * 1024 * 1024),
     )(*results)
 
 

time: 64.4 us -> 61.3 us (0.952)
  Pallas kernels: 63.5 us -> 60.5 us
    pallas_call x1, Pallas kernels: 61.6 us -> 59.6 us  [per_device(): pl.pallas_call(functools.partial(attention_kernel, sizes), out_shape=(jax...]
    pallas_call x1, Pallas kernels: 1.91 us -> 0.92 us  [per_device(): pl.pallas_call(hand_over, out_shape=tuple((jax.ShapeDtypeStruct(x.shape,...]
where the time goes in v3:
time: 61.3 us; the launch traced here: 61.1 us
  Pallas kernels  60.5 us (99%)
  between operations  0.64 us (1%)
    pallas_call x1, Pallas kernels, per_device(): pl.pallas_call(functools.partial(attention_kernel, sizes), out_shape=(jax...  59.6 us

profile of v3, /device:TPU:1, one launch (start us, length us, event | category | flops | bytes accessed | tf_op | source)
XLA Modules:
  0.0 61.1 jit_solution(7257625563725691815)
XLA Ops:
  0.6 59.6 %shard_map.68 = (bf16[48,8192]{1,0:T(8,128)(2,1)S(1)}, f32[8,384]{1,0:T(8,128)S(1)}) custom-call(bf16[48,8192]{1,0:T(8,128)(2,1)} %q_ref.1, bf16[48,1024]{1,0:T(8,128)(2,1)} %k_ref.1, bf16[48,1024]{1,0:T(8,128)(2,1)} %v_ref.1, s32[384,128]{1,0:T(8,128)} %bitcast.2, s32[3,128]{1,0:T(4,128)} %bitcast.3), custom_call_target="tpu_custom_call" | custom-call | tf_op jit(solution)/shard_map/pallas_call | solution.py:402
  60.2 0.9 %shard_map.69 = (bf16[48,8192]{1,0:T(8,128)(2,1)}, f32[8,384]{1,0:T(8,128)}) custom-call(bf16[48,8192]{1,0:T(8,128)(2,1)S(1)} %get-tuple-element.4.mixed_ref, f32[8,384]{1,0:T(8,128)S(1)} %get-tuple-element.5.log_in_ref), custom_call_target="tpu_custom_call" | custom-call | tf_op jit(solution)/shard_map/pallas_call | solution.py:434

commit v4 on v3

--- a/solution.py
+++ b/solution.py
@@ -15,6 +15,8 @@
 EARLY_CHUNKS = 1
 QUERY_TILE = 192
 MASKED = -1e30
+NEAR = (0, 3)
+FAR = (1, 2)
 HAND_OVER_PARTS = 3
 MESH = pl.DeviceIdType.MESH
 
@@ -33,6 +35,8 @@
     o_buf,
     bias,
     logs,
+    first_top,
+    first_mixed,
     place,
     plan,
     local_sem,
@@ -42,10 +46,14 @@
     next_recv,
     relay_send,
     relay_recv,
+    block_sem,
+    go,
     q_send,
     q_recv,
     o_send,
     o_recv,
+    first_send,
+    first_recv,
 ):
     heads, inners, outers = sizes
     rows = q_ref.shape[0]
@@ -124,29 +132,37 @@
     def next_copies(r, act):
         @pl.when(even)
         def _():
-            act(next_copy(both, 1, r))
             act(next_copy(both, 0, r))
 
         @pl.when(jnp.logical_not(even))
         def _():
-            act(next_copy(0, 0, r))
-            act(next_copy(1, 1, r))
+            act(next_copy(both, 1, r))
 
         act(next_copy(both, 2, r))
 
-    def whole_landing(r):
-        return arrival(piece(both, 2 - side, r), relay_send.at[r], next_recv.at[1 - side, r])
-
-    def half_landing(r):
-        return arrival(piece(side, 1 + side, r), relay_send.at[r], next_recv.at[side, r])
+    def block_copy():
+        return pltpu.make_async_remote_copy(
+            src_ref=kv_buf.at[:, 0, :, key_value],
+            dst_ref=kv_buf.at[:, 2, :, key_value],
+            send_sem=block_sem.at[0],
+            recv_sem=block_sem.at[1],
+            device_id=targets[1],
+            device_id_type=MESH,
+        )
+
+    def near_landing(r):
+        return arrival(piece(both, 1, r), relay_send.at[r], next_recv.at[0, r])
+
+    def far_landing(r):
+        return arrival(piece(both, 2, r), relay_send.at[r], next_recv.at[1, r])
 
     def outer_landing(r):
         return arrival(piece(both, 3, r), relay_send.at[r], next_recv.at[2, r])
 
     def relay_copy(r):
         return pltpu.make_async_remote_copy(
-            src_ref=piece(side, 1 + side, r),
-            dst_ref=piece(side, 2 - side, r),
+            src_ref=piece(both, 2, r),
+            dst_ref=piece(both, 1, r),
             send_sem=relay_send.at[r],
             recv_sem=relay_recv.at[r],
             device_id=partner,
@@ -154,7 +170,7 @@
         )
 
     def relay_landing(r):
-        return arrival(piece(1 - side, 1 + side, r), relay_send.at[r], relay_recv.at[r])
+        return arrival(piece(both, 1, r), relay_send.at[r], relay_recv.at[r])
 
     def q_columns(owner, c):
         return pl.ds(pl.multiple_of(owner * (GROUP * WIDTH) + c * wide, WIDTH), wide)
@@ -201,6 +217,31 @@
             recv_sem=o_recv.at[c, r],
             device_id={"head": peer(r)},
             device_id_type=MESH,
+        )
+
+    def head_columns(owner, j):
+        return pl.ds(pl.multiple_of((owner * GROUP + j) * WIDTH, WIDTH), WIDTH)
+
+    def first_copy(j, r):
+        to = peer(r)
+        return pltpu.make_async_remote_copy(
+            src_ref=o_buf.at[0, row_span(to), pl.ds(j * WIDTH, WIDTH)],
+            dst_ref=out_ref.at[:, head_columns(me, j)],
+            send_sem=first_send.at[j, r],
+            recv_sem=first_recv.at[j, r],
+            device_id={"head": to},
+            device_id_type=MESH,
+        )
+
+    def first_landing(j, r):
+        part = out_ref.at[:, head_columns(lax.rem(me + heads - r, heads), j)]
+        return arrival(part, first_send.at[j, r], first_recv.at[j, r])
+
+    def own_first(j):
+        return pltpu.make_async_copy(
+            o_buf.at[0, row_span(me), pl.ds(j * WIDTH, WIDTH)],
+            out_ref.at[:, head_columns(me, j)],
+            first_send.at[j, 0],
         )
 
     own_kv = [
@@ -231,10 +272,8 @@
         pl.semaphore_signal(barrier, inc=1, device_id={"head": peer(r)}, device_id_type=MESH)
     for origin in origins:
         pl.semaphore_signal(barrier, inc=1, device_id=origin, device_id_type=MESH)
-    for copy in own_kv + tables:
+    for copy in own_kv:
         copy.start()
-    for c in range(chunks):
-        own_q(c).start()
     pl.semaphore_wait(barrier, len(offsets) + len(origins))
 
     for r in offsets[::-1]:
@@ -243,6 +282,8 @@
 
     for copy in own_kv:
         copy.wait()
+    for copy in tables:
+        copy.start()
     next_copies(0, lambda copy: copy.start())
     for c in range(EARLY_CHUNKS):
         for r in offsets:
@@ -254,6 +295,8 @@
         for r in offsets:
             q_copy(c, r).start()
 
+    for c in range(chunks):
+        own_q(c).start()
     for copy in tables:
         copy.wait()
     here = inner * outers + outer
@@ -294,77 +337,142 @@
     kv_buf[1, :, :, WIDTH:] = jnp.ones((STEPS, block_rows, LANES), kv_buf.dtype)
     logs[...] = jnp.zeros_like(logs)
 
+    scale = WIDTH**-0.5
+    exponent = scale * 1.4426950408889634
+
+    def one_head(c, j, finish):
+        for tile in range(0, block_rows, QUERY_TILE):
+            span = slice(tile, tile + QUERY_TILE)
+            query = q_buf[c, span, j * WIDTH : (j + 1) * WIDTH]
+            finish(c, j, span, query)
+
+    def fold(query, span, steps, prior=None):
+        scores = [
+            lax.dot_general(
+                query,
+                kv_buf[0, step, :, :WIDTH],
+                (((1,), (1,)), ((), ())),
+                preferred_element_type=jnp.float32,
+            )
+            + bias[span, step * block_rows : (step + 1) * block_rows]
+            for step in steps
+        ]
+        top = functools.reduce(jnp.maximum, scores)
+        top = jnp.max(top, axis=1, keepdims=True)
+        mixed = jnp.zeros((QUERY_TILE, 2 * WIDTH), jnp.float32)
+        if prior is not None:
+            before, mixed = prior
+            top = jnp.maximum(top, before)
+            mixed = mixed * jnp.exp2((before - top) * exponent)
+        for score, step in zip(scores, steps):
+            weights = jnp.exp2((score - top) * exponent)
+            mixed += jnp.dot(
+                weights.astype(jnp.bfloat16),
+                kv_buf[1, step],
+                preferred_element_type=jnp.float32,
+            )
+        return top, mixed
+
+    def write(c, j, span, top, mixed):
+        total = mixed[:, WIDTH:]
+        o_buf[c, span, j * WIDTH : (j + 1) * WIDTH] = (mixed[:, :WIDTH] / total).astype(
+            o_buf.dtype
+        )
+        lane = lax.broadcasted_iota(jnp.int32, (QUERY_TILE, LANES), 1)
+        logs[span, :] = jnp.where(
+            lane == c * CHUNK_HEADS + j, top * scale + jnp.log(total), logs[span, :]
+        )
+
+    def near_part(c, j, span, query):
+        top, mixed = fold(query, span, NEAR)
+        first_top[span, :] = jnp.broadcast_to(top, (QUERY_TILE, LANES))
+        first_mixed[span, :] = mixed
+
+    def far_part(c, j, span, query):
+        prior = (first_top[span, :1], first_mixed[span, :])
+        write(c, j, span, *fold(query, span, FAR, prior))
+
+    def whole(c, j, span, query):
+        write(c, j, span, *fold(query, span, range(STEPS)))
+
+    def take_queries(c):
+        own_q(c).wait()
+        for r in offsets:
+            q_landing(c, r).wait_recv()
+
     @pl.when(jnp.logical_not(even))
     def _():
-        whole_landing(0).wait_recv()
-
-    for r in pieces:
-        half_landing(r).wait_recv()
-        relay_copy(r).start()
+        for r in pieces:
+            next_copy(both, 1, r).wait_send()
+        near_landing(0).wait_recv()
+        pl.semaphore_signal(go, inc=1, device_id=partner, device_id_type=MESH)
+
+    @pl.when(even)
+    def _():
+        pl.semaphore_wait(go, 1)
+        block_copy().start()
+
     for r in pieces:
         outer_landing(r).wait_recv()
-        if r:
-            whole_landing(r).wait_recv()
+    take_queries(0)
+    one_head(0, 0, near_part)
+
+    @pl.when(jnp.logical_not(even))
+    def _():
+        for r in pieces[1:]:
+            near_landing(r).wait_recv()
+        for r in pieces:
+            far_landing(r).wait_recv()
+            relay_copy(r).start()
 
     @pl.when(even)
     def _():
-        whole_landing(0).wait_recv()
-
-    for r in pieces:
-        relay_landing(r).wait_recv()
-
-    scale = WIDTH**-0.5
-    exponent = scale * 1.4426950408889634
+        for r in pieces:
+            relay_landing(r).wait_recv()
+        block_copy().wait_recv()
+
+    for j in range(CHUNK_HEADS):
+        one_head(0, j, whole if j else far_part)
+        own_first(j).start()
+        for r in offsets:
+            first_copy(j, r).start()
 
     def one_chunk(c, carry):
-        own_q(c).wait()
-        for r in offsets:
-            q_landing(c, r).wait_recv()
+        take_queries(c)
         for j in range(CHUNK_HEADS):
-            columns = slice(j * WIDTH, (j + 1) * WIDTH)
-            for tile in range(0, block_rows, QUERY_TILE):
-                span = slice(tile, tile + QUERY_TILE)
-                query = q_buf[c, span, columns]
-                scores = [
-                    lax.dot_general(
-                        query,
-                        kv_buf[0, step, :, :WIDTH],
-                        (((1,), (1,)), ((), ())),
-                        preferred_element_type=jnp.float32,
-                    )
-                    + bias[span, step * block_rows : (step + 1) * block_rows]
-                    for step in range(STEPS)
-                ]
-                top = functools.reduce(jnp.maximum, scores)
-                top = jnp.max(top, axis=1, keepdims=True)
-                mixed = jnp.zeros((QUERY_TILE, 2 * WIDTH), jnp.float32)
-                for step in range(STEPS):
-                    weights = jnp.exp2((scores[step] - top) * exponent)
-                    mixed += jnp.dot(
-                        weights.astype(jnp.bfloat16),
-                        kv_buf[1, step],
-                        preferred_element_type=jnp.float32,
-                    )
-                total = mixed[:, WIDTH:]
-                o_buf[c, span, columns] = (mixed[:, :WIDTH] / total).astype(o_buf.dtype)
-                lane = lax.broadcasted_iota(jnp.int32, (QUERY_TILE, LANES), 1)
-                logs[span, :] = jnp.where(
-                    lane == c * CHUNK_HEADS + j, top * scale + jnp.log(total), logs[span, :]
-                )
+            one_head(c, j, whole)
         own_o(c).start()
         for r in offsets:
             o_copy(c, r).start()
         return carry
 
-    lax.fori_loop(0, chunks, one_chunk, 0)
+    lax.fori_loop(1, chunks, one_chunk, 0)
     log_ref[...] = jnp.transpose(logs[...])[:GROUP]
 
     for r in pieces:
         if r:
             kv_landing(r).wait_send()
-        next_copies(r, lambda copy: copy.wait_send())
-        relay_copy(r).wait_send()
-    for c in range(chunks):
+        next_copy(both, 2, r).wait_send()
+
+    @pl.when(even)
+    def _():
+        for r in pieces:
+            next_copy(both, 0, r).wait_send()
+        block_copy().wait_send()
+
+    @pl.when(jnp.logical_not(even))
+    def _():
+        for r in pieces:
+            relay_copy(r).wait_send()
+
+    for j in range(CHUNK_HEADS):
+        own_first(j).wait()
+        for r in offsets:
+            first_copy(j, r).wait_send()
+            first_landing(j, r).wait_recv()
+    for r in offsets:
+        q_copy(0, r).wait_send()
+    for c in range(1, chunks):
         own_o(c).wait()
         for r in offsets:
             q_copy(c, r).wait_send()
@@ -413,6 +521,8 @@
             pltpu.VMEM((chunks, block_rows, CHUNK_HEADS * WIDTH), kind),
             pltpu.VMEM((block_rows, STEPS * block_rows), jnp.float32),
             pltpu.VMEM((block_rows, LANES), jnp.float32),
+            pltpu.VMEM((block_rows, LANES), jnp.float32),
+            pltpu.VMEM((block_rows, 2 * WIDTH), jnp.float32),
             pltpu.VMEM(place.shape, jnp.int32),
             pltpu.VMEM(used.shape, jnp.int32),
             dma((4,)),
@@ -422,10 +532,14 @@
             dma((STEPS - 1, heads)),
             dma((heads,)),
             dma((heads,)),
+            dma((2,)),
+            pltpu.SemaphoreType.REGULAR,
             dma((chunks, heads)),
             dma((chunks, heads)),
             dma((chunks, heads)),
             dma((chunks, heads)),
+            dma((CHUNK_HEADS, heads)),
+            dma((CHUNK_HEADS, heads)),
         ],
         compiler_params=pltpu.CompilerParams(
             collective_id=0, has_side_effects=True, vmem_limit_bytes=30 * 1024 * 1024

time: 61.3 us -> 56.9 us (0.928)
  the two profiles are of different devices: /device:TPU:1 before, /device:TPU:16 now
where the time goes in v4:
time: 56.9 us; the launch traced here: 56.7 us
  Pallas kernels  56.1 us (99%)
  between operations  0.64 us (1%)
    pallas_call x1, Pallas kernels, per_device(): pl.pallas_call(functools.partial(attention_kernel, sizes), out_shape=(jax...  55.2 us

profile of v4, /device:TPU:16, one launch (start us, length us, event | category | flops | bytes accessed | tf_op | source)
XLA Modules:
  0.0 56.7 jit_solution(13303237173643566686)
XLA Ops:
  0.6 55.2 %shard_map.68 = (bf16[48,8192]{1,0:T(8,128)(2,1)S(1)}, f32[8,384]{1,0:T(8,128)S(1)}) custom-call(bf16[48,8192]{1,0:T(8,128)(2,1)} %q_ref.1, bf16[48,1024]{1,0:T(8,128)(2,1)} %k_ref.1, bf16[48,1024]{1,0:T(8,128)(2,1)} %v_ref.1, s32[384,128]{1,0:T(8,128)} %bitcast.2, s32[3,128]{1,0:T(4,128)} %bitcast.3), custom_call_target="tpu_custom_call" | custom-call | tf_op jit(solution)/shard_map/pallas_call | solution.py:510
  55.8 0.9 %shard_map.69 = (bf16[48,8192]{1,0:T(8,128)(2,1)}, f32[8,384]{1,0:T(8,128)}) custom-call(bf16[48,8192]{1,0:T(8,128)(2,1)S(1)} %get-tuple-element.4.mixed_ref, f32[8,384]{1,0:T(8,128)S(1)} %get-tuple-element.5.log_in_ref), custom_call_target="tpu_custom_call" | custom-call | tf_op jit(solution)/shard_map/pallas_call | solution.py:548

commit v5 on v4

--- a/solution.py
+++ b/solution.py
@@ -48,6 +48,7 @@
     relay_recv,
     block_sem,
     go,
+    ready,
     q_send,
     q_recv,
     o_send,
@@ -68,6 +69,7 @@
     pieces = [0] + offsets[::-1]
     side = lax.rem(inner, 2)
     even = side == 0
+    first_cycle = inner < 2
 
     def peer(r):
         return lax.rem(me + r, heads)
@@ -80,12 +82,12 @@
         {"inner": lax.rem(inner + 2, inners)},
         {"outer": lax.rem(outer + 1, outers)},
     )
-    origins = (
-        {"inner": lax.rem(inner + inners - 1, inners)},
-        {"inner": lax.rem(inner + inners - 2, inners)},
-        {"outer": lax.rem(outer + outers - 1, outers)},
-    )
-
+    outer_origin = {"outer": lax.rem(outer + outers - 1, outers)}
+    inner_origin = {"inner": lax.rem(inner + inners - 2, inners)}
+    wraps = inner >= inners - 2
+    wrapped = inner < 2
+    second = jnp.logical_and(wraps, even)
+    ahead = jnp.logical_not(jnp.logical_or(wraps, even))
     partner = {"inner": inner + 1 - 2 * side}
     key_value = pl.ds(0, WIDTH)
 
@@ -270,11 +272,73 @@
     barrier = pltpu.get_barrier_semaphore()
     for r in offsets:
         pl.semaphore_signal(barrier, inc=1, device_id={"head": peer(r)}, device_id_type=MESH)
-    for origin in origins:
-        pl.semaphore_signal(barrier, inc=1, device_id=origin, device_id_type=MESH)
-    for copy in own_kv:
+    pl.semaphore_signal(barrier, inc=1, device_id=outer_origin, device_id_type=MESH)
+
+    @pl.when(jnp.logical_not(even))
+    def _():
+        pl.semaphore_signal(barrier, inc=1, device_id=partner, device_id_type=MESH)
+
+    @pl.when(wrapped)
+    def _():
+        pl.semaphore_signal(barrier, inc=1, device_id=inner_origin, device_id_type=MESH)
+
+    @pl.when(jnp.logical_not(wraps))
+    def _():
+        pl.semaphore_signal(barrier, inc=1, device_id=targets[1], device_id_type=MESH)
+
+    for copy in own_kv + tables:
         copy.start()
-    pl.semaphore_wait(barrier, len(offsets) + len(origins))
+    in_last = lax.div(inner, inners - 2)
+    in_first = lax.div(inners - 1 - inner, inners - 2)
+    pl.semaphore_wait(barrier, len(offsets) + 1 + (1 - side) + in_last + (1 - in_first))
+
+    @pl.when(jnp.logical_not(wrapped))
+    def _():
+        pl.semaphore_signal(ready, inc=1, device_id=inner_origin, device_id_type=MESH)
+
+
+    def make_mask():
+        for copy in tables:
+            copy.wait()
+        here = inner * outers + outer
+        sources = (
+            here,
+            lax.rem(inner + inners - 1, inners) * outers + outer,
+            lax.rem(inner + inners - 2, inners) * outers + outer,
+            inner * outers + lax.rem(outer + outers - 1, outers),
+        )
+        def starts(block):
+            first = block * block_rows
+            second = first + run
+            out = []
+            for spot in (first, second):
+                line = place[pl.ds(lax.div(spot, LANES), 1), :]
+                lane = lax.broadcasted_iota(jnp.int32, (1, LANES), 1)
+                out.append(
+                    jnp.sum(
+                        jnp.where(lane == lax.rem(spot, LANES), line, 0), axis=1, keepdims=True
+                    )
+                )
+            return out
+
+        lane = lax.broadcasted_iota(jnp.int32, plan.shape, 1)
+        used = jnp.max(jnp.where(lane == here, plan[...], 0), axis=1, keepdims=True)
+        q_first, q_second = starts(here)
+        q_row = lax.broadcasted_iota(jnp.int32, (block_rows, 1), 0)
+        q_place = jnp.where(q_row < run, q_first + q_row, q_second + q_row - run)
+        k_row = lax.broadcasted_iota(jnp.int32, (1, block_rows), 1)
+        for step, source in enumerate(sources):
+            k_first, k_second = starts(source)
+            k_place = jnp.where(k_row < run, k_first + k_row, k_second + k_row - run)
+            if step:
+                k_place = jnp.where(used[step - 1 : step] == 1, k_place, jnp.int32(2**30))
+            bias[:, step * block_rows : (step + 1) * block_rows] = jnp.where(
+                k_place <= q_place, jnp.float32(0), jnp.float32(MASKED)
+            )
+
+    @pl.when(second)
+    def _():
+        make_mask()
 
     for r in offsets[::-1]:
         kv_copy(0, r).start()
@@ -282,58 +346,38 @@
 
     for copy in own_kv:
         copy.wait()
-    for copy in tables:
-        copy.start()
-    next_copies(0, lambda copy: copy.start())
     for c in range(EARLY_CHUNKS):
         for r in offsets:
             q_copy(c, r).start()
+
+    @pl.when(ahead)
+    def _():
+        for c in range(EARLY_CHUNKS, chunks):
+            for r in offsets:
+                q_copy(c, r).start()
+
+    @pl.when(ahead)
+    def _():
+        pl.semaphore_wait(ready, 1)
+
+    next_copies(0, lambda copy: copy.start())
     for r in pieces[1:]:
         kv_landing(r).wait_recv()
         next_copies(r, lambda copy: copy.start())
-    for c in range(EARLY_CHUNKS, chunks):
-        for r in offsets:
-            q_copy(c, r).start()
+
+    @pl.when(jnp.logical_not(ahead))
+    def _():
+        for c in range(EARLY_CHUNKS, chunks):
+            for r in offsets:
+                q_copy(c, r).start()
+
 
     for c in range(chunks):
         own_q(c).start()
-    for copy in tables:
-        copy.wait()
-    here = inner * outers + outer
-    sources = (
-        here,
-        lax.rem(inner + inners - 1, inners) * outers + outer,
-        lax.rem(inner + inners - 2, inners) * outers + outer,
-        inner * outers + lax.rem(outer + outers - 1, outers),
-    )
-    def starts(block):
-        first = block * block_rows
-        second = first + run
-        out = []
-        for spot in (first, second):
-            line = place[pl.ds(lax.div(spot, LANES), 1), :]
-            lane = lax.broadcasted_iota(jnp.int32, (1, LANES), 1)
-            out.append(
-                jnp.sum(
-                    jnp.where(lane == lax.rem(spot, LANES), line, 0), axis=1, keepdims=True
-                )
-            )
-        return out
-
-    lane = lax.broadcasted_iota(jnp.int32, plan.shape, 1)
-    used = jnp.max(jnp.where(lane == here, plan[...], 0), axis=1, keepdims=True)
-    q_first, q_second = starts(here)
-    q_row = lax.broadcasted_iota(jnp.int32, (block_rows, 1), 0)
-    q_place = jnp.where(q_row < run, q_first + q_row, q_second + q_row - run)
-    k_row = lax.broadcasted_iota(jnp.int32, (1, block_rows), 1)
-    for step, source in enumerate(sources):
-        k_first, k_second = starts(source)
-        k_place = jnp.where(k_row < run, k_first + k_row, k_second + k_row - run)
-        if step:
-            k_place = jnp.where(used[step - 1 : step] == 1, k_place, jnp.int32(2**30))
-        bias[:, step * block_rows : (step + 1) * block_rows] = jnp.where(
-            k_place <= q_place, jnp.float32(0), jnp.float32(MASKED)
-        )
+    @pl.when(jnp.logical_not(second))
+    def _():
+        make_mask()
+
     kv_buf[1, :, :, WIDTH:] = jnp.ones((STEPS, block_rows, LANES), kv_buf.dtype)
     logs[...] = jnp.zeros_like(logs)
 
@@ -385,11 +429,11 @@
 
     def near_part(c, j, span, query):
         top, mixed = fold(query, span, NEAR)
-        first_top[span, :] = jnp.broadcast_to(top, (QUERY_TILE, LANES))
-        first_mixed[span, :] = mixed
+        first_top[c, j, span, :] = jnp.broadcast_to(top, (QUERY_TILE, LANES))
+        first_mixed[c, j, span, :] = mixed
 
     def far_part(c, j, span, query):
-        prior = (first_top[span, :1], first_mixed[span, :])
+        prior = (first_top[c, j, span, :1], first_mixed[c, j, span, :])
         write(c, j, span, *fold(query, span, FAR, prior))
 
     def whole(c, j, span, query):
@@ -402,20 +446,41 @@
 
     @pl.when(jnp.logical_not(even))
     def _():
-        for r in pieces:
+        near_landing(0).wait_recv()
+        for r in pieces[:-3]:
             next_copy(both, 1, r).wait_send()
-        near_landing(0).wait_recv()
         pl.semaphore_signal(go, inc=1, device_id=partner, device_id_type=MESH)
+        for r in pieces[-3:]:
+            next_copy(both, 1, r).wait_send()
 
     @pl.when(even)
     def _():
         pl.semaphore_wait(go, 1)
+
+        @pl.when(jnp.logical_not(wraps))
+        def _():
+            pl.semaphore_wait(ready, 1)
+
         block_copy().start()
 
     for r in pieces:
         outer_landing(r).wait_recv()
     take_queries(0)
     one_head(0, 0, near_part)
+
+    @pl.when(first_cycle)
+    def _():
+        for j in range(1, CHUNK_HEADS):
+            one_head(0, j, near_part)
+
+        def near_chunk(c, carry):
+            take_queries(c)
+            for j in range(CHUNK_HEADS):
+                one_head(c, j, near_part)
+            return carry
+
+        lax.fori_loop(1, chunks, near_chunk, 0)
+
 
     @pl.when(jnp.logical_not(even))
     def _():
@@ -432,15 +497,34 @@
         block_copy().wait_recv()
 
     for j in range(CHUNK_HEADS):
-        one_head(0, j, whole if j else far_part)
+        if j:
+
+            @pl.when(first_cycle)
+            def _():
+                one_head(0, j, far_part)
+
+            @pl.when(jnp.logical_not(first_cycle))
+            def _():
+                one_head(0, j, whole)
+
+        else:
+            one_head(0, j, far_part)
         own_first(j).start()
         for r in offsets:
             first_copy(j, r).start()
 
     def one_chunk(c, carry):
-        take_queries(c)
-        for j in range(CHUNK_HEADS):
-            one_head(c, j, whole)
+        @pl.when(first_cycle)
+        def _():
+            for j in range(CHUNK_HEADS):
+                one_head(c, j, far_part)
+
+        @pl.when(jnp.logical_not(first_cycle))
+        def _():
+            take_queries(c)
+            for j in range(CHUNK_HEADS):
+                one_head(c, j, whole)
+
         own_o(c).start()
         for r in offsets:
             o_copy(c, r).start()
@@ -521,8 +605,8 @@
             pltpu.VMEM((chunks, block_rows, CHUNK_HEADS * WIDTH), kind),
             pltpu.VMEM((block_rows, STEPS * block_rows), jnp.float32),
             pltpu.VMEM((block_rows, LANES), jnp.float32),
-            pltpu.VMEM((block_rows, LANES), jnp.float32),
-            pltpu.VMEM((block_rows, 2 * WIDTH), jnp.float32),
+            pltpu.VMEM((chunks, CHUNK_HEADS, block_rows, LANES), jnp.float32),
+            pltpu.VMEM((chunks, CHUNK_HEADS, block_rows, 2 * WIDTH), jnp.float32),
             pltpu.VMEM(place.shape, jnp.int32),
             pltpu.VMEM(used.shape, jnp.int32),
             dma((4,)),
@@ -533,6 +617,7 @@
             dma((heads,)),
             dma((heads,)),
             dma((2,)),
+            pltpu.SemaphoreType.REGULAR,
             pltpu.SemaphoreType.REGULAR,
             dma((chunks, heads)),
             dma((chunks, heads)),

time: 56.9 us -> 57 us (level)
  the two profiles are of different devices: /device:TPU:16 before, /device:TPU:1 now
where the time goes in v5:
time: 57 us; the launch traced here: 56.3 us
  Pallas kernels  55.5 us (97%)
  between operations  0.8 us (1%)
    pallas_call x1, Pallas kernels, per_device(): pl.pallas_call(functools.partial(attention_kernel, sizes), out_shape=(jax...  54.6 us

profile of v5, /device:TPU:1, one launch (start us, length us, event | category | flops | bytes accessed | tf_op | source)
XLA Modules:
  0.0 56.3 jit_solution(12953335237358965040)
XLA Ops:
  0.6 54.6 %shard_map.68 = (bf16[48,8192]{1,0:T(8,128)(2,1)S(1)}, f32[8,384]{1,0:T(8,128)S(1)}) custom-call(bf16[48,8192]{1,0:T(8,128)(2,1)} %q_ref.1, bf16[48,1024]{1,0:T(8,128)(2,1)} %k_ref.1, bf16[48,1024]{1,0:T(8,128)(2,1)} %v_ref.1, s32[384,128]{1,0:T(8,128)} %bitcast.2, s32[3,128]{1,0:T(4,128)} %bitcast.3), custom_call_target="tpu_custom_call" | custom-call | tf_op jit(solution)/shard_map/pallas_call | solution.py:594
  55.2 0.9 %shard_map.69 = (bf16[48,8192]{1,0:T(8,128)(2,1)}, f32[8,384]{1,0:T(8,128)}) custom-call(bf16[48,8192]{1,0:T(8,128)(2,1)S(1)} %get-tuple-element.4.mixed_ref, f32[8,384]{1,0:T(8,128)S(1)} %get-tuple-element.5.log_in_ref), custom_call_target="tpu_custom_call" | custom-call | tf_op jit(solution)/shard_map/pallas_call | solution.py:633
